TPU v7x, 32 devices: a whole 2x2x4 slice. The times are simulated.
32 devices in a mesh: shot: 2 (over y), row: 4 (over x, core), freq: 4 (over z).
Axes of the slice: x: 2, y: 2, z: 4, core: 2. Of those that a mesh axis runs over, the one named last changes fastest.
Arguments:
- source_field: float32 [2, 8, 1024, 1024], P(None, ('shot', 'freq'), 'row'), parts along dimension 1, may hold values from -6 to 6
- receiver_field: float32 [2, 8, 1024, 1024], P(None, ('shot', 'freq'), 'row'), parts along dimension 1, may hold values from -6 to 6
- slowness: float32 [4, 1024, 1024], P('freq', 'row'), may hold values from 0.22 to 0.67
- owner: int32 [4], replicated, may hold values from 0 to 3, each once
- freq_index: int32 [8], P(('shot', 'freq')), parts along dimension 0, may hold values from 0 to 3, each once
Outputs:
- source_out: float32 [2, 8, 1024, 1024], P(None, ('shot', 'freq'), 'row'), parts along dimension 1
- receiver_out: float32 [2, 8, 1024, 1024], P(None, ('shot', 'freq'), 'row'), parts along dimension 1
- image: float32 [4, 1024, 1024], P('shot', 'row', 'freq'), parts along dimension 0
There are 2 independent parts, one for each index of `shot`. A program takes and returns all parts, laid end to end along the dimension named above; an argument that names none is the same for every part. Nothing has to cross between parts.
All inputs are finite; a program needn't handle non-finite values.
Results may differ from a plain program's by a relative error of at most 0.00022.
Values sent between devices are 32-bit elements; how exact they have to be, the bound alone decides.
A program may use at most 128 MiB of HBM per device.

v0:
```python
import math
import jax
import jax.numpy as jnp
from jax import lax
from jax.sharding import PartitionSpec as P

NZ = 2
dz_km = 0.01
dx_km = 0.0125
ref_slow = 0.5
base_hertz = 3.0
step_hertz = 4.0
taper = 0.5


def spread(value, axis, source):
    kept = jnp.where(lax.axis_index(axis) == source, value, 0).astype(value.dtype)
    return lax.psum(kept, axis)


def split_length(length):
    return length // 128


def angle_table(count_a, count_b, modulus, sign):
    left = jnp.arange(count_a, dtype=jnp.int32)[:, None]
    right = jnp.arange(count_b, dtype=jnp.int32)[None, :]
    turns = (left * right % modulus).astype(jnp.float32) * (2.0 * math.pi / modulus)
    return (jnp.cos(turns), sign * jnp.sin(turns))


def contract(form, left, right):
    return jnp.einsum(form, left, right, precision=lax.Precision.HIGHEST)


def transform_pair(real_part, imag_part, sign, last):
    length = real_part.shape[2] if last else real_part.shape[1]
    first = split_length(length)
    second = length // first
    cos_a, sin_a = angle_table(first, first, first, sign)
    cos_b, sin_b = angle_table(second, second, second, sign)
    twist_c, twist_s = angle_table(first, second, length, sign)
    if last:
        shape = (real_part.shape[0], real_part.shape[1], first, second)
        form_one = "fajb,jk->fakb"
        form_two = "fakb,bm->famk"
    else:
        shape = (real_part.shape[0], first, second, real_part.shape[2])
        form_one = "fjbq,jk->fkbq"
        form_two = "fkbq,bm->fmkq"
        twist_c = twist_c[:, :, None]
        twist_s = twist_s[:, :, None]
    x_re = real_part.reshape(shape)
    x_im = imag_part.reshape(shape)
    y_re = contract(form_one, x_re, cos_a) - contract(form_one, x_im, sin_a)
    y_im = contract(form_one, x_im, cos_a) + contract(form_one, x_re, sin_a)
    z_re = y_re * twist_c - y_im * twist_s
    z_im = y_im * twist_c + y_re * twist_s
    out_re = contract(form_two, z_re, cos_b) - contract(form_two, z_im, sin_b)
    out_im = contract(form_two, z_im, cos_b) + contract(form_two, z_re, sin_b)
    return (out_re.reshape(real_part.shape), out_im.reshape(real_part.shape))


def transform(block, sign, last):
    count = block.shape[0]
    freqs = block.shape[2]
    plane = block.shape[3:]
    real_part = block[:, 0].reshape((count * freqs,) + plane)
    imag_part = block[:, 1].reshape((count * freqs,) + plane)
    out_re, out_im = transform_pair(real_part, imag_part, sign, last)
    shape = (count, freqs) + plane
    return jnp.stack([out_re.reshape(shape), out_im.reshape(shape)], axis=1)


def wavenumbers(length, start, count):
    index = start + jnp.arange(count, dtype=jnp.int32)
    signed = jnp.where(index * 2 < length, index, index - length)
    return signed.astype(jnp.float32) * (2.0 * math.pi / (length * dx_km))


def rotate(block, cos_v, sin_v):
    real_part = block[:, 0]
    imag_part = block[:, 1]
    return jnp.stack(
        [real_part * cos_v - imag_part * sin_v, imag_part * cos_v + real_part * sin_v], axis=1
    )


def shift_phase(block, omega, kx_part, ky_part, total):
    square = kx_part[:, None] ** 2 + ky_part[None, :] ** 2
    kmax = math.pi / dx_km
    damp = jnp.exp(-taper * square / (kmax * kmax)) / total
    ws0 = omega[:, None, None] * ref_slow
    vertical = ws0 - 0.5 * square[None] / ws0
    cos_v = jnp.cos(dz_km * vertical) * damp
    sin_v = jnp.sin(dz_km * vertical) * damp
    return rotate(block, cos_v, sin_v)


def correct(block, slab, omega):
    theta = omega[:, None, None] * (slab[None] - ref_slow) * dz_km
    return rotate(block, jnp.cos(theta), jnp.sin(theta))


def image_term(block):
    return jnp.sum(block[0, 0] * block[1, 0] - block[0, 1] * block[1, 1], axis=0)


def body(source_field, receiver_field, slowness, owner, freq_index):
    rows = source_field.shape[2]
    width = source_field.shape[3]
    row_count = lax.axis_size("row")
    height = rows * row_count
    cols = width // row_count
    place = lax.axis_index("row")
    omega = 2.0 * math.pi * (base_hertz + step_hertz * freq_index.astype(jnp.float32))
    mirrored = jnp.stack([receiver_field[0], -receiver_field[1]])
    fields = jnp.stack([source_field, mirrored])
    kx_all = wavenumbers(height, 0, height)
    ky_own = wavenumbers(width, place * cols, cols)
    total = float(height * width)
    slab_dev = slowness.shape[0]
    images = []
    for depth in range(NZ):
        chosen = owner[depth]
        held = spread(slowness, "freq", chosen // slab_dev)
        slab = lax.dynamic_index_in_dim(held, chosen % slab_dev, 0, keepdims=False)
        fields = transform(fields, -1.0, True)
        fields = lax.all_to_all(fields, "row", split_axis=4, concat_axis=3, tiled=True)
        items = fields
        items = transform(items, -1.0, False)
        items = shift_phase(items, omega, kx_all, ky_own, total)
        fields = transform(items, 1.0, False)
        fields = lax.all_to_all(fields, "row", split_axis=3, concat_axis=4, tiled=True)
        fields = transform(fields, 1.0, True)
        fields = correct(fields, slab, omega)
        images.append(image_term(fields))
    parts = [lax.psum_scatter(term, "freq", scatter_dimension=1, tiled=True) for term in images]
    image = jnp.stack(parts)
    source_out = fields[0]
    receiver_out = jnp.stack([fields[1, 0], -fields[1, 1]])
    return (source_out, receiver_out, image)


def solution(mesh):
    in_specs = (
        P(None, ("shot", "freq"), "row", None),
        P(None, ("shot", "freq"), "row", None),
        P("freq", "row", None),
        P(),
        P(("shot", "freq")),
    )
    out_specs = (
        P(None, ("shot", "freq"), "row", None),
        P(None, ("shot", "freq"), "row", None),
        P("shot", "row", "freq"),
    )
    return jax.shard_map(body, mesh=mesh, in_specs=in_specs, out_specs=out_specs, check_vma=False)
```

profile of v0, /device:TPU:0, one launch (start us, length us, event | category | flops | bytes accessed | tf_op | source)
XLA Modules:
  0.0 596.2 jit_solution(643073891319918496)
XLA Ops:
  20.3 2.7 fusion.112
  32.7 5.4 copy.346
  38.1 4.9 all-to-all-start
  44.0 4.0 fusion.186
  48.1 43.7 %all-to-all-done = f32[2,2,1,256,1024]{3,0,2,1,4:T(2,128)} async-done(((f32[2,2,1,256,1024]{3,0,2,1,4:T(2,128)}), f32[2,2,1,256,1024]{3,0,2,1,4:T(2,128)}, u32[]{:S(2)}, u32[]{:S(2)}) %all-to-all-start) | async-done | bytes 4194336 | tf_op jit(solution)/shard_map/all_to_all | solution.py:129
  91.8 5.0 copy.347
  96.7 5.4 copy.348
  104.7 2.9 fusion.104
  107.6 2.9 fusion.102
  110.5 2.9 fusion.118
  113.4 3.8 subtract_bitcast_fusion.13
  122.4 2.6 subtract_bitcast_fusion.12
  126.3 2.6 add_bitcast_fusion.12
  131.0 2.9 fusion.88
  133.9 2.9 fusion.86
  136.8 3.0 fusion.124
  139.8 3.9 subtract_bitcast_fusion.11
  143.7 2.6 fusion.80
  148.9 2.6 subtract_bitcast_fusion.10
  152.8 2.8 add_bitcast_fusion.10
  157.1 5.2 copy.372
  162.4 5.0 all-to-all-start.1
  171.0 90.0 %all-reduce.3.cloned.1.call-done = (f32[1,256,1024]{2,1,0:T(8,128)}, f32[1,256,1024]{2,1,0:T(8,128)}) async-done(((f32[1,256,1024]{2,1,0:T(8,128)}, f32[1,256,1024]{2,1,0:T(8,128)}), (f32[1,256,1024]{2,1,0:T(8,128)}, f32[1,256,1024]{2,1,0:T(8,128)})) %all-reduce.3.cloned.1.call-update) | async-done | bytes 2097168 | tf_op jit(solution)/shard_map/psum | solution.py:18
  260.9 4.7 fusion.192
  268.6 5.0 copy.373
  273.6 5.3 copy.374
  278.9 4.6 fusion.663
  285.6 3.2 fusion.318
  301.9 2.8 subtract_bitcast_fusion.8
  312.5 2.9 copy.386
  315.4 4.8 fusion.314
  320.2 3.1 copy.385
  323.3 3.6 fusion.316
  343.5 3.2 copy.395
  346.8 50.7 %all_to_all.72 = f32[2,2,1,256,1024]{3,0,2,1,4:T(2,128)S(1)} all-to-all(f32[2,2,1,256,1024]{3,0,2,1,4:T(2,128)S(1)} %copy.395), channel_id=1, replica_groups=mesh['shot'=2,'row'=4,'freq'=4] {'row'}, dimensions={4} | all-to-all | bytes 8388608 | tf_op jit(solution)/shard_map/all_to_all | solution.py:129
  397.5 2.7 copy.396
  400.3 5.7 copy.397
  408.5 2.9 fusion.56
  411.4 2.9 fusion.54
  414.3 2.9 fusion.130
  417.2 3.6 subtract_bitcast_fusion.5
  426.0 2.6 subtract_bitcast_fusion.4
  429.8 2.6 add_bitcast_fusion.4
  434.6 2.9 fusion.40
  437.5 2.9 fusion.38
  440.3 3.0 fusion.136
  443.4 4.0 subtract_bitcast_fusion.3
  447.4 2.6 fusion.32
  452.5 2.6 subtract_bitcast_fusion.2
  456.4 2.8 add_bitcast_fusion.2
  460.8 5.2 copy.418
  466.0 4.9 all-to-all-start.3
  471.0 2.6 copy.436
  474.9 5.7 cosine_bitcast_fusion
  484.7 4.7 fusion.10
  490.7 28.5 %all-to-all-done.3 = f32[2,2,1,1024,256]{4,0,2,1,3:T(2,128)} async-done(((f32[2,2,1,1024,256]{4,0,2,1,3:T(2,128)}), f32[2,2,1,1024,256]{4,0,2,1,3:T(2,128)}, u32[]{:S(2)}, u32[]{:S(2)}) %all-to-all-start.3) | async-done | bytes 4194336 | tf_op jit(solution)/shard_map/all_to_all | solution.py:134
  519.2 5.0 copy.419
  524.2 5.3 copy.420
  529.4 4.6 fusion.661
  536.1 3.2 fusion.306
  562.1 3.0 pad_maximum_fusion.6
  565.1 3.0 copy.444
  568.1 4.3 fusion.14
  574.3 13.1 %reduce-scatter.5.cloned.1.call-done = f32[256,256]{0,1:T(8,128)} async-done(((f32[256,1024]{0,1:T(8,128)}), f32[256,256]{0,1:T(8,128)}) %reduce-scatter.5.cloned.1.call-update) | async-done | bytes 262160 | tf_op jit(solution)/shard_map/reduce_scatter | solution.py:138
  (137 shorter events, 135.5 us)
Async XLA Ops:
  8.9 1.6 copy-start.19
  38.1 53.7 %all-to-all-start = ((f32[2,2,1,256,1024]{3,0,2,1,4:T(2,128)}), f32[2,2,1,256,1024]{3,0,2,1,4:T(2,128)}, u32[]{:S(2)}, u32[]{:S(2)}) async-start(f32[2,2,1,256,1024]{3,0,2,1,4:T(2,128)} %copy.346), calls=%async_computation | async-start | bytes 8388608 | tf_op jit(solution)/shard_map/all_to_all | solution.py:129
  48.1 82.2 %copy-start.8 = (f32[8,128,256]{2,1,0:T(8,128)}, f32[8,128,256]{2,1,0:T(8,128)S(1)}, u32[]{:S(2)}) copy-start(f32[8,128,256]{2,1,0:T(8,128)S(1)} %get-tuple-element.67) | copy-start | bytes 3145732
  162.4 5.1 copy-start.21
  162.4 7.0 %copy-start.20 = (f32[1,256,1024]{2,1,0:T(8,128)S(1)}, f32[1,256,1024]{2,1,0:T(8,128)}, u32[]{:S(2)}) copy-start(f32[1,256,1024]{2,1,0:T(8,128)} %param.7) | copy-start | bytes 3145732
  162.4 106.2 %all-to-all-start.1 = ((f32[2,2,1,1024,256]{4,0,2,1,3:T(2,128)}), f32[2,2,1,1024,256]{4,0,2,1,3:T(2,128)}, u32[]{:S(2)}, u32[]{:S(2)}) async-start(f32[2,2,1,1024,256]{4,0,2,1,3:T(2,128)} %copy.372), calls=%async_computation.1 | async-start | bytes 8388608 | tf_op jit(solution)/shard_map/all_to_all | solution.py:134
  167.4 93.5 %all-reduce.3.cloned.1.call-start = ((), (), s32[]{:S(2)}) async-start(), calls=%async_computation.8 | async-start | bytes 4194304 | tf_op jit(solution)/shard_map/psum | solution.py:18
  265.7 2.9 copy-start.11
  265.7 2.9 copy-start.13
  285.6 3.2 copy-start.6
  291.1 1.9 copy-start.14
  293.0 2.0 copy-start.7
  307.1 1.3 copy-start.1
  308.4 1.2 copy-start.17
  308.4 1.5 copy-start.18
  323.2 3.6 copy-start.2
  323.3 3.6 copy-start.15
  326.9 2.0 copy-start.5
  432.6 1.2 copy-start.9
  466.0 53.1 %all-to-all-start.3 = ((f32[2,2,1,1024,256]{4,0,2,1,3:T(2,128)}), f32[2,2,1,1024,256]{4,0,2,1,3:T(2,128)}, u32[]{:S(2)}, u32[]{:S(2)}) async-start(f32[2,2,1,1024,256]{4,0,2,1,3:T(2,128)} %copy.418), calls=%async_computation.3 | async-start | bytes 8388608 | tf_op jit(solution)/shard_map/all_to_all | solution.py:134
  470.9 2.7 copy-start.12
  470.9 103.4 %reduce-scatter.3.cloned.1.call-start = ((), (), s32[]{:S(2)}) async-start(), calls=%async_computation.6 | async-start | bytes 1310720 | tf_op jit(solution)/shard_map/reduce_scatter | solution.py:138
  490.7 96.8 %reduce-scatter.5.cloned.1.call-start = ((), (), s32[]{:S(2)}) async-start(), calls=%async_computation.7 | async-start | bytes 1310720 | tf_op jit(solution)/shard_map/reduce_scatter | solution.py:138
  536.1 3.2 copy-start.3
  541.8 1.9 copy-start.16
  543.7 2.0 copy-start.4
  555.2 2.3 copy-start.10
  557.5 2.5 copy-start
Sparse Core Ops, SparseCore 0:
  171.2 89.6 all-reduce.2
  490.8 26.5 reduce-scatter.2
  562.2 25.1 reduce-scatter.4
where the time goes:
time: 606 us; the launch traced here: 596 us
  waiting for transfers between devices  175 us (29%)
  matrix products  170 us (28%)
  local copies, waits for them, and re-layouts  125 us (21%)
  blocking collectives  50.7 us (8%)
  other arithmetic  42.9 us (7%)
  between operations  17.4 us (3%)
  starting transfers between devices  14.9 us (2%)
    dot_general x64, matrix products, contract(): return jnp.einsum(form, left, right, precision=lax.Precision.HIGHEST)  170 us
    psum x1, waiting for transfers between devices, spread(): return lax.psum(kept, axis)  90 us
    all_to_all x1, blocking collectives, body(): lax.all_to_all(fields, 'row', split_axis=4, concat_axis=3, tiled=True)  50.7 us
    all_to_all x1, waiting for transfers between devices, body(): lax.all_to_all(fields, 'row', split_axis=4, concat_axis=3, tiled=True)  43.7 us
    all_to_all x2, waiting for transfers between devices, body(): lax.all_to_all(fields, 'row', split_axis=3, concat_axis=4, tiled=True)  28.5 us
    all_to_all x4, local copies, waits for them, and re-layouts, body(): lax.all_to_all(fields, 'row', split_axis=3, concat_axis=4, tiled=True)  20.5 us
    another operation x4, local copies, waits for them, and re-layouts, transform(): return jnp.stack([out_re.reshape(shape), out_im.reshape(shape)], axis=1)  19.1 us
    all_to_all x4, local copies, waits for them, and re-layouts, body(): lax.all_to_all(fields, 'row', split_axis=4, concat_axis=3, tiled=True)  18.9 us
  transfers between devices with their start and end apart: 6, of which 4 were waited for; matrix products, arithmetic and copies ran while one was open for 15% of the time, Pallas kernels for 0%

commit v1 on v0

--- a/solution.py
+++ b/solution.py
@@ -15,7 +15,7 @@
 
 def spread(value, axis, source):
     kept = jnp.where(lax.axis_index(axis) == source, value, 0).astype(value.dtype)
-    return lax.psum(kept, axis)
+    return jnp.sum(lax.all_gather(kept, axis), axis=0)
 
 
 def split_length(length):

time: 606 us -> 580 us (0.957)
  waiting for transfers between devices: 175 us -> 145 us
  other arithmetic: 42.9 us -> 49.5 us
    psum x1 -> x0, waiting for transfers between devices: 90 us -> none  [spread(): return lax.psum(kept, axis)]
    all_to_all x2, waiting for transfers between devices: 28.5 us -> 87.5 us  [body(): lax.all_to_all(fields, 'row', split_axis=3, concat_axis=4, tiled=True)]
    mul x6 -> x0, local copies, waits for them, and re-layouts: 10.9 us -> none  [the longest x3 5.76 us: rotate(): real_part * cos_v - imag_part * sin_v]
    reduce_sum x0 -> x2, other arithmetic: none -> 7.38 us  [spread(): return jnp.sum(lax.all_gather(kept, axis), axis=0)]
  transfers between devices with their start and end apart: 6 -> 7, of which waited for: 4 -> 4; matrix products, arithmetic and copies ran while one was open for 15% -> 32% of each run, Pallas kernels for 0% -> 0%
where the time goes in v1:
time: 580 us; the launch traced here: 570 us
  matrix products  171 us (29%)
  waiting for transfers between devices  145 us (25%)
  local copies, waits for them, and re-layouts  122 us (21%)
  blocking collectives  50.7 us (9%)
  other arithmetic  49.5 us (9%)
  between operations  17.5 us (3%)
  starting transfers between devices  15 us (3%)
    dot_general x64, matrix products, contract(): return jnp.einsum(form, left, right, precision=lax.Precision.HIGHEST)  171 us
    all_to_all x2, waiting for transfers between devices, body(): lax.all_to_all(fields, 'row', split_axis=3, concat_axis=4, tiled=True)  87.5 us
    all_to_all x1, blocking collectives, body(): lax.all_to_all(fields, 'row', split_axis=4, concat_axis=3, tiled=True)  50.7 us
    all_to_all x1, waiting for transfers between devices, body(): lax.all_to_all(fields, 'row', split_axis=4, concat_axis=3, tiled=True)  40.2 us
    all_to_all x4, local copies, waits for them, and re-layouts, body(): lax.all_to_all(fields, 'row', split_axis=3, concat_axis=4, tiled=True)  20.5 us
    another operation x4, local copies, waits for them, and re-layouts, transform(): return jnp.stack([out_re.reshape(shape), out_im.reshape(shape)], axis=1)  19.4 us
    all_to_all x4, local copies, waits for them, and re-layouts, body(): lax.all_to_all(fields, 'row', split_axis=4, concat_axis=3, tiled=True)  18.8 us
    reduce_scatter x2, waiting for transfers between devices, body(): lax.psum_scatter(term, 'freq', scatter_dimension=1, tiled=True)  16 us
  transfers between devices with their start and end apart: 7, of which 4 were waited for; matrix products, arithmetic and copies ran while one was open for 32% of the time, Pallas kernels for 0%

profile of v1, /device:TPU:0, one launch (start us, length us, event | category | flops | bytes accessed | tf_op | source)
XLA Modules:
  0.0 569.8 jit_solution(4685522784400157122)
XLA Ops:
  32.4 5.8 %copy.330 = f32[2,2,1,256,1024]{3,0,2,1,4:T(2,128)} copy(f32[2,2,1,256,1024]{3,4,0,2,1:T(8,128)S(1)} %pad_maximum_fusion) | data formatting | bytes 8388608 | tf_op jit(solution)/shard_map/stack | solution.py:72
  38.2 5.0 all-to-all-start
  47.8 4.1 fusion.186
  51.9 40.2 %all-to-all-done = f32[2,2,1,256,1024]{3,0,2,1,4:T(2,128)} async-done(((f32[2,2,1,256,1024]{3,0,2,1,4:T(2,128)}), f32[2,2,1,256,1024]{3,0,2,1,4:T(2,128)}, u32[]{:S(2)}, u32[]{:S(2)}) %all-to-all-start) | async-done | bytes 4194336 | tf_op jit(solution)/shard_map/all_to_all | solution.py:129
  92.1 5.1 copy.331
  97.2 5.5 copy.332
  105.2 2.9 fusion.104
  108.1 2.9 fusion.102
  111.0 3.0 fusion.118
  114.0 3.7 subtract_bitcast_fusion.13
  120.3 2.6 subtract_bitcast_fusion.12
  126.7 2.6 add_bitcast_fusion.12
  131.7 2.9 fusion.88
  134.6 2.9 fusion.86
  137.4 3.0 fusion.124
  140.5 3.7 subtract_bitcast_fusion.11
  144.2 2.6 fusion.80
  146.8 2.6 subtract_bitcast_fusion.10
  153.2 2.8 add_bitcast_fusion.10
  157.6 5.2 copy.356
  162.7 4.8 all-to-all-start.1
  168.3 47.5 %all-to-all-done.1 = f32[2,2,1,1024,256]{4,0,2,1,3:T(2,128)} async-done(((f32[2,2,1,1024,256]{4,0,2,1,3:T(2,128)}), f32[2,2,1,1024,256]{4,0,2,1,3:T(2,128)}, u32[]{:S(2)}, u32[]{:S(2)}) %all-to-all-start.1) | async-done | bytes 4194336 | tf_op jit(solution)/shard_map/all_to_all | solution.py:134
  215.8 5.0 copy.357
  220.8 5.3 copy.358
  226.1 4.0 fusion.665
  234.4 3.7 reduce.2
  238.1 3.4 fusion.320
  255.0 3.7 add_bitcast_fusion.8
  258.6 3.7 reduce.3
  262.3 9.8 %fusion.192 = (f32[256,1024]{1,0:T(8,128)}, f32[256,1024]{1,0:T(8,128)}, f32[256,1024]{1,0:T(8,128)}, f32[256,1024]{1,0:T(8,128)}) fusion(f32[256,1024]{1,0:T(8,128)} %reduce.2, f32[]{:T(128)} %bitcast.53, f32[256,1024]{1,0:T(8,128)} %reduce.3), kind=kLoop, calls=%fused_computation.230 | loop fusion | flops 1572864 | bytes 6291460 | tf_op jit(solution)/shard_map/cos | solution.py:102
  282.9 2.9 copy.370
  285.8 4.8 fusion.316
  290.6 3.3 copy.369
  293.9 3.6 fusion.318
  314.1 3.2 copy.379
  317.4 50.7 %all_to_all.72 = f32[2,2,1,256,1024]{3,0,2,1,4:T(2,128)S(1)} all-to-all(f32[2,2,1,256,1024]{3,0,2,1,4:T(2,128)S(1)} %copy.379), channel_id=1, replica_groups=mesh['shot'=2,'row'=4,'freq'=4] {'row'}, dimensions={4} | all-to-all | bytes 8388608 | tf_op jit(solution)/shard_map/all_to_all | solution.py:129
  368.1 2.7 copy.380
  370.8 5.5 copy.381
  378.9 2.9 fusion.56
  381.8 2.9 fusion.54
  384.6 2.9 fusion.130
  387.6 3.8 subtract_bitcast_fusion.5
  396.6 2.6 subtract_bitcast_fusion.4
  400.4 2.6 add_bitcast_fusion.4
  405.1 2.9 fusion.40
  408.0 2.9 fusion.38
  410.9 3.0 fusion.136
  413.9 3.9 subtract_bitcast_fusion.3
  417.9 2.6 fusion.32
  423.1 2.6 subtract_bitcast_fusion.2
  426.9 2.8 add_bitcast_fusion.2
  431.3 5.3 copy.402
  436.6 5.0 all-to-all-start.3
  441.6 4.3 fusion.10
  449.7 40.1 %all-to-all-done.3 = f32[2,2,1,1024,256]{4,0,2,1,3:T(2,128)} async-done(((f32[2,2,1,1024,256]{4,0,2,1,3:T(2,128)}), f32[2,2,1,1024,256]{4,0,2,1,3:T(2,128)}, u32[]{:S(2)}, u32[]{:S(2)}) %all-to-all-start.3) | async-done | bytes 4194336 | tf_op jit(solution)/shard_map/all_to_all | solution.py:134
  489.8 5.0 copy.403
  494.8 5.2 copy.404
  500.1 4.6 fusion.663
  506.8 3.2 fusion.308
  523.1 2.8 subtract_bitcast_fusion
  532.7 3.0 pad_maximum_fusion.6
  535.8 2.9 copy.428
  538.6 4.5 fusion.14
  545.1 16.0 %reduce-scatter.5.cloned.1.call-done = f32[256,256]{0,1:T(8,128)} async-done(((f32[256,1024]{0,1:T(8,128)}), f32[256,256]{0,1:T(8,128)}) %reduce-scatter.5.cloned.1.call-update) | async-done | bytes 262160 | tf_op jit(solution)/shard_map/reduce_scatter | solution.py:138
  (135 shorter events, 135.6 us)
Async XLA Ops:
  8.9 1.6 copy-start.17
  38.2 5.1 copy-start.19
  38.2 7.0 %copy-start.18 = (f32[1,256,1024]{2,1,0:T(8,128)S(1)}, f32[1,256,1024]{2,1,0:T(8,128)}, u32[]{:S(2)}) copy-start(f32[1,256,1024]{2,1,0:T(8,128)} %param.7) | copy-start | bytes 3145732
  38.2 53.9 %all-to-all-start = ((f32[2,2,1,256,1024]{3,0,2,1,4:T(2,128)}), f32[2,2,1,256,1024]{3,0,2,1,4:T(2,128)}, u32[]{:S(2)}, u32[]{:S(2)}) async-start(f32[2,2,1,256,1024]{3,0,2,1,4:T(2,128)} %copy.330), calls=%async_computation | async-start | bytes 8388608 | tf_op jit(solution)/shard_map/all_to_all | solution.py:129
  43.2 191.2 %all-gather.5.cloned.1.call-start = ((), (), s32[]{:S(2)}) async-start(), calls=%async_computation.8 | async-start | bytes 5242880 | tf_op jit(solution)/shard_map/all_gather | solution.py:18
  51.9 79.1 %copy-start.7 = (f32[8,128,256]{2,1,0:T(8,128)}, f32[8,128,256]{2,1,0:T(8,128)S(1)}, u32[]{:S(2)}) copy-start(f32[8,128,256]{2,1,0:T(8,128)S(1)} %get-tuple-element.65) | copy-start | bytes 3145732
  162.7 53.1 %all-to-all-start.1 = ((f32[2,2,1,1024,256]{4,0,2,1,3:T(2,128)}), f32[2,2,1,1024,256]{4,0,2,1,3:T(2,128)}, u32[]{:S(2)}, u32[]{:S(2)}) async-start(f32[2,2,1,1024,256]{4,0,2,1,3:T(2,128)} %copy.356), calls=%async_computation.1 | async-start | bytes 8388608 | tf_op jit(solution)/shard_map/all_to_all | solution.py:134
  167.6 91.0 %all-gather.7.cloned.1.call-start = ((), (), s32[]{:S(2)}) async-start(), calls=%async_computation.9 | async-start | bytes 5242880 | tf_op jit(solution)/shard_map/all_gather | solution.py:18
  243.4 2.0 copy-start.3
  277.2 1.6 copy-start.1
  278.8 1.2 copy-start.9
  278.8 1.5 copy-start.11
  293.9 3.6 copy-start.2
  293.9 3.6 copy-start.13
  297.5 2.0 copy-start.6
  403.2 1.2 copy-start.8
  436.6 5.1 copy-start.10
  436.6 53.2 %all-to-all-start.3 = ((f32[2,2,1,1024,256]{4,0,2,1,3:T(2,128)}), f32[2,2,1,1024,256]{4,0,2,1,3:T(2,128)}, u32[]{:S(2)}, u32[]{:S(2)}) async-start(f32[2,2,1,1024,256]{4,0,2,1,3:T(2,128)} %copy.402), calls=%async_computation.3 | async-start | bytes 8388608 | tf_op jit(solution)/shard_map/all_to_all | solution.py:134
  441.6 103.5 %reduce-scatter.3.cloned.1.call-start = ((), (), s32[]{:S(2)}) async-start(), calls=%async_computation.6 | async-start | bytes 1310720 | tf_op jit(solution)/shard_map/reduce_scatter | solution.py:138
  446.0 1.3 copy-start.16
  447.2 1.2 copy-start.15
  447.2 113.8 %reduce-scatter.5.cloned.1.call-start = ((), (), s32[]{:S(2)}) async-start(), calls=%async_computation.7 | async-start | bytes 1310720 | tf_op jit(solution)/shard_map/reduce_scatter | solution.py:138
  506.8 3.2 copy-start.4
  512.3 1.9 copy-start.14
  514.2 2.0 copy-start.5
  525.9 2.3 copy-start.12
  528.2 2.5 copy-start
Sparse Core Ops, SparseCore 0:
  46.9 83.8 all-gather.4
  170.0 83.2 all-gather.6
  447.4 29.5 reduce-scatter.2
  532.9 28.1 reduce-scatter.4
